TPU v7x, 128 devices: a whole 4x4x4 slice. The times are simulated.
128 devices in a mesh: row: 8 (over y, core), col: 16 (over x, z).
Axes of the slice: x: 4, y: 4, z: 4, core: 2. Of those that a mesh axis runs over, the one named last changes fastest.
Arguments:
- tensor_tiles: bfloat16 [512, 128, 128, 128], P(('row', 'col')), may hold values from -384 to 384
- tile_mode1: int32 [512], P(('row', 'col')), may hold values from 0 to 1023, as said below
- tile_mode2: int32 [512], P(('row', 'col')), may hold values from 0 to 127
- tile_mode3: int32 [512], P(('row', 'col')), may hold values from 0 to 63
- factor_mode2: bfloat16 [48, 16384], P(None, 'col'), may hold values from -1 to 1
- factor_mode3: bfloat16 [48, 8192], P(None, 'row'), may hold values from -1 to 1
Outputs:
- factor_mode1: float32 [48, 131072], P(None, ('row', 'col'))
Inputs may be any that keep to these rules, and one draw needn't show every extreme that they name: `tile_mode1`: tiles at positions g*64 to (g+1)*64 - 1 have mode-1 blocks in g*128 to (g+1)*128 - 1; the 4 tiles at positions d*4 to (d+1)*4 - 1 have mode-1 blocks in distinct groups of 8 consecutive blocks (block // 8 all different).
All inputs are finite; a program needn't handle non-finite values.
Results may differ from a plain program's by a relative error of at most 0.0003.
Values may be sent and summed in bfloat16 or wider, within the bound.
No kernel may reach another device: no remote copies, remote signals or barrier semaphores. Data moves between devices by JAX's collectives and lax.ppermute only.
A program may use at most 128 MiB of HBM per device.

v0:
```python
import jax
import jax.numpy as jnp
from jax import lax
from jax.sharding import PartitionSpec as P

IB_DEV = 8
ridge_term = 0.5


def body(tensor_tiles, tile_mode1, tile_mode2, tile_mode3, factor_mode2, factor_mode3):
    rank_count = factor_mode2.shape[0]
    tile_edge = tensor_tiles.shape[1]
    gram_two = lax.psum(
        jnp.dot(factor_mode2, factor_mode2.T, preferred_element_type=jnp.float32), "col"
    )
    gram_three = lax.psum(
        jnp.dot(factor_mode3, factor_mode3.T, preferred_element_type=jnp.float32), "row"
    )
    system = gram_two * gram_three + ridge_term * jnp.eye(rank_count, dtype=jnp.float32)
    full_two = lax.all_gather(factor_mode2, "col", axis=1, tiled=True)
    full_three = lax.all_gather(factor_mode3, "row", axis=1, tiled=True)
    mode2_rows = jnp.transpose(
        full_two.reshape(rank_count, -1, tile_edge)[:, tile_mode2], (1, 0, 2)
    )
    mode3_rows = jnp.transpose(
        full_three.reshape(rank_count, -1, tile_edge)[:, tile_mode3], (1, 0, 2)
    )
    contracted = jnp.einsum(
        "trc,tabc->trab", mode3_rows, tensor_tiles, preferred_element_type=jnp.float32
    )
    tile_rows = jnp.einsum(
        "trab,trb->tra", contracted, mode2_rows.astype(jnp.float32), precision=lax.Precision.HIGHEST
    )
    col_count = lax.axis_size("col")
    row_blocks = IB_DEV * col_count
    local_blocks = tile_mode1 - lax.axis_index("row") * row_blocks
    selector = (local_blocks[:, None] == jnp.arange(row_blocks, dtype=jnp.int32)[None, :]).astype(
        jnp.float32
    )
    row_partials = jnp.einsum("tra,tb->rba", tile_rows, selector, precision=lax.Precision.HIGHEST)
    row_partials = row_partials.reshape(rank_count, row_blocks * tile_edge)
    right_side = lax.psum_scatter(row_partials, "col", scatter_dimension=1, tiled=True)
    cholesky_factor = jnp.linalg.cholesky(system)
    middle = lax.linalg.triangular_solve(cholesky_factor, right_side, left_side=True, lower=True)
    return lax.linalg.triangular_solve(
        cholesky_factor, middle, left_side=True, lower=True, transpose_a=True
    )


def solution(mesh):
    in_specs = (
        P(("row", "col"), None, None, None),
        P(("row", "col")),
        P(("row", "col")),
        P(("row", "col")),
        P(None, "col"),
        P(None, "row"),
    )
    out_specs = P(None, ("row", "col"))
    return jax.shard_map(body, mesh=mesh, in_specs=in_specs, out_specs=out_specs, check_vma=False)
```

profile of v0, /device:TPU:0, one launch (start us, length us, event | category | flops | bytes accessed | tf_op | source)
XLA Modules:
  0.0 194.9 jit_solution(6708601685298031785)
XLA Ops:
  6.5 0.0 all-gather.2.cloned.1.call-start
  6.5 0.7 all-gather.2.cloned.1.call-update
  7.3 0.0 reduce-scatter.2.cloned.1.call-start
  7.3 0.7 compare_select_fusion.1
  8.0 14.2 %all_gather.6 = bf16[48,8192]{1,0:T(8,128)(2,1)S(1)} all-gather(bf16[48,1024]{1,0:T(8,128)(2,1)} %param.11), channel_id=1, replica_groups=mesh['row'=8,'col'=16] {'row'}, dimensions={1}, use_global_device_ids=true | all-gather | bytes 884736 | tf_op jit(solution)/shard_map/all_gather | solution.py:21
  22.2 0.1 copy_bitcast_fusion.2
  22.3 0.6 gather_fusion
  22.9 0.7 compare_select_fusion
  23.6 0.7 broadcast_subtract_fusion
  24.2 12.1 %fusion.6 = f32[4,48,128,128]{3,1,2,0:T(8,128)} fusion(bf16[4,128,128,128]{3,2,1,0:T(8,128)(2,1)} %param.6, bf16[4,48,128]{2,1,0:T(8,128)(2,1)S(1)} %gather_fusion), kind=kOutput, calls=%fused_computation.11 | convolution fusion | flops 805306368 | bytes 29409280 | tf_op jit(solution)/shard_map/trc,tabc->trab/dot_general | solution.py:28
  36.3 19.6 %all-gather.2.cloned.1.call-done = bf16[48,16384]{1,0:T(8,128)(2,1)} async-done(((bf16[48,1024]{1,0:T(8,128)(2,1)}), bf16[48,16384]{1,0:T(8,128)(2,1)}) %all-gather.2.cloned.1.call-update) | async-done | bytes 1572880 | tf_op jit(solution)/shard_map/all_gather | solution.py:20
  55.9 1.7 copy_bitcast_fusion.1
  57.6 0.6 gather_fusion.1
  58.1 0.0 copy-start.1
  58.1 0.0 copy-start
  58.2 16.7 %fusion = f32[4,48,1,128]{3,2,1,0:T(1,128)S(1)} fusion(f32[4,48,128,128]{3,1,2,0:T(8,128)} %fusion.6, bf16[4,48,128,1]{2,1,0,3:T(8,128)(2,1)S(1)} %bitcast.47), kind=kOutput, calls=%fused_computation.2 | convolution fusion | flops 37748736 | bytes 12730368 | tf_op jit(solution)/shard_map/trab,trb->tra/dot_general | solution.py:31
  74.9 1.5 fusion.2
  76.4 3.5 %copy.30 = f32[6,8,128,128]{3,1,2,0:T(8,128)} copy(f32[6,8,128,128]{3,2,1,0:T(8,128)S(1)} %bitcast.46) | data formatting | bytes 6291456
  79.8 0.0 reduce-scatter.2.cloned.1.call-update
  79.9 0.0 copy-done.1
  79.9 0.1 fusion.17
  80.0 72.5 %psum.14 = f32[48,48]{1,0:T(8,128)S(1)} all-reduce(f32[48,48]{1,0:T(8,128)S(1)} %fusion.17), channel_id=1, replica_groups=mesh['row'=8,'col'=16] {'col'}, use_global_device_ids=true, to_apply=%region_0.0 | all-reduce | flops 2304 | bytes 18432 | tf_op jit(solution)/shard_map/psum | solution.py:13
  152.5 0.0 copy-done
  152.5 0.1 fusion.18
  152.7 23.6 %psum.15 = f32[48,48]{1,0:T(8,128)S(1)} all-reduce(f32[48,48]{1,0:T(8,128)S(1)} %fusion.18), channel_id=1, replica_groups=mesh['row'=8,'col'=16] {'row'}, use_global_device_ids=true, to_apply=%region_1.0 | all-reduce | flops 2304 | bytes 18432 | tf_op jit(solution)/shard_map/psum | solution.py:16
  176.3 0.1 copy.9
  176.4 4.4 %cholesky.16 = f32[48,48]{1,0:T(8,128)S(1)} custom-call(f32[48,48]{1,0:T(8,128)S(1)} %fusion.13), custom_call_target="Cholesky" | custom-call | tf_op jit(solution)/shard_map/jit(cholesky)/cholesky | solution.py:43
  180.8 0.6 compare_reduce_fusion
  181.4 0.7 fusion.8
  182.1 3.7 %custom-call.8 = f32[1,48,48]{1,2,0:T(8,128)S(1)} custom-call(f32[1,48,48]{2,1,0:T(8,128)S(1)} %fusion.8), custom_call_target="InvertDiagBlocksLowerTriangular" | custom-call | tf_op jit(solution)/shard_map/triangular_solve | solution.py:45
  185.8 1.3 fusion.11
  187.1 1.0 fusion.9
  (6 shorter events, 0.1 us)
Async XLA Ops:
  6.5 49.4 %all-gather.2.cloned.1.call-start = ((), (), s32[]{:S(2)}) async-start(), calls=%async_computation.1 | async-start | bytes 1671168 | tf_op jit(solution)/shard_map/all_gather | solution.py:20
  7.3 178.5 %reduce-scatter.2.cloned.1.call-start = ((), (), s32[]{:S(2)}) async-start(), calls=%async_computation.2 | async-start | bytes 3342336 | tf_op jit(solution)/shard_map/reduce_scatter | solution.py:42
  58.1 21.7 %copy-start.1 = (bf16[48,1024]{1,0:T(8,128)(2,1)S(1)}, bf16[48,1024]{1,0:T(8,128)(2,1)}, u32[]{:S(2)}) copy-start(bf16[48,1024]{1,0:T(8,128)(2,1)} %param.10) | copy-start | bytes 294916
  58.1 94.4 %copy-start = (bf16[48,1024]{1,0:T(8,128)(2,1)S(1)}, bf16[48,1024]{1,0:T(8,128)(2,1)}, u32[]{:S(2)}) copy-start(bf16[48,1024]{1,0:T(8,128)(2,1)} %param.11) | copy-start | bytes 294916
Sparse Core Ops, SparseCore 0:
  9.5 46.3 all-gather.1
  80.0 76.1 reduce-scatter.1
where the time goes:
time: 195 us
  blocking collectives  110 us (56%)
  matrix products  32.8 us (17%)
  waiting for transfers between devices  20.3 us (10%)
  between operations  13.5 us (7%)
  other arithmetic  11.4 us (6%)
  local copies, waits for them, and re-layouts  6.49 us (3%)
    psum x1, blocking collectives, body(): lax.psum(jnp.dot(factor_mode2, factor_mode2.T, preferred_element_type=jnp...  72.5 us
    psum x1, blocking collectives, body(): lax.psum(jnp.dot(factor_mode3, factor_mode3.T, preferred_element_type=jnp...  23.6 us
    all_gather x1, waiting for transfers between devices, body(): full_two = lax.all_gather(factor_mode2, 'col', axis=1, tiled=True)  19.6 us
    dot_general x1, matrix products, body(): jnp.einsum('trab,trb->tra', contracted, mode2_rows.astype(jnp.float32), p...  16.7 us
    all_gather x1, blocking collectives, body(): full_three = lax.all_gather(factor_mode3, 'row', axis=1, tiled=True)  14.2 us
    dot_general x1, matrix products, body(): jnp.einsum('trc,tabc->trab', mode3_rows, tensor_tiles, preferred_element_...  12.1 us
    another operation x3, other arithmetic, body(): cholesky_factor = jnp.linalg.cholesky(system)  5.05 us
    another operation x2, other arithmetic, body(): lax.linalg.triangular_solve(cholesky_factor, middle, left_side=True, lowe...  4.32 us
  transfers between devices with their start and end apart: 2, of which 1 were waited for; matrix products, arithmetic and copies ran while one was open for 13% of the time, Pallas kernels for 0%

commit v1 on v0

--- a/solution.py
+++ b/solution.py
@@ -17,7 +17,9 @@
         jnp.dot(factor_mode3, factor_mode3.T, preferred_element_type=jnp.float32), "row"
     )
     system = gram_two * gram_three + ridge_term * jnp.eye(rank_count, dtype=jnp.float32)
-    full_two = lax.all_gather(factor_mode2, "col", axis=1, tiled=True)
+    full_two = jnp.concatenate(
+        lax.all_to_all(jnp.stack([factor_mode2] * lax.axis_size("col")), "col", 0, 0), axis=1
+    )
     full_three = lax.all_gather(factor_mode3, "row", axis=1, tiled=True)
     mode2_rows = jnp.transpose(
         full_two.reshape(rank_count, -1, tile_edge)[:, tile_mode2], (1, 0, 2)

time: 195 us -> 188 us (0.964)
  waiting for transfers between devices: 20.3 us -> 0.02 us
  starting transfers between devices: 0.04 us -> 8.03 us
  local copies, waits for them, and re-layouts: 6.49 us -> 9.7 us
  blocking collectives: 110 us -> 113 us
    all_gather x1 -> x0, waiting for transfers between devices: 19.6 us -> none  [body(): full_two = lax.all_gather(factor_mode2, 'col', axis=1, tiled=True)]
    all_to_all x0 -> x1, starting transfers between devices: none -> 7.99 us  [body(): lax.all_to_all(jnp.stack([factor_mode2] * lax.axis_size('col')), 'col', 0...]
    another operation x0 -> x3, local copies, waits for them, and re-layouts: none -> 4.03 us  [the longest x1 2.28 us: body(): jnp.stack([factor_mode2] * lax.axis_size('col'))]
    psum x1, blocking collectives: 72.5 us -> 74.9 us  [body(): lax.psum(jnp.dot(factor_mode2, factor_mode2.T, preferred_element_type=jnp...]
  transfers between devices with their start and end apart: 2 -> 2, of which waited for: 1 -> 0; matrix products, arithmetic and copies ran while one was open for 13% -> 13% of each run, Pallas kernels for 0% -> 0%
where the time goes in v1:
time: 188 us
  blocking collectives  113 us (60%)
  matrix products  32.8 us (17%)
  between operations  13.6 us (7%)
  other arithmetic  11.4 us (6%)
  local copies, waits for them, and re-layouts  9.7 us (5%)
  starting transfers between devices  8.03 us (4%)
    psum x1, blocking collectives, body(): lax.psum(jnp.dot(factor_mode2, factor_mode2.T, preferred_element_type=jnp...  74.9 us
    psum x1, blocking collectives, body(): lax.psum(jnp.dot(factor_mode3, factor_mode3.T, preferred_element_type=jnp...  23.6 us
    dot_general x1, matrix products, body(): jnp.einsum('trab,trb->tra', contracted, mode2_rows.astype(jnp.float32), p...  16.7 us
    all_gather x1, blocking collectives, body(): full_three = lax.all_gather(factor_mode3, 'row', axis=1, tiled=True)  14.1 us
    dot_general x1, matrix products, body(): jnp.einsum('trc,tabc->trab', mode3_rows, tensor_tiles, preferred_element_...  12.1 us
    all_to_all x1, starting transfers between devices, body(): lax.all_to_all(jnp.stack([factor_mode2] * lax.axis_size('col')), 'col', 0...  7.99 us
    another operation x3, other arithmetic, body(): cholesky_factor = jnp.linalg.cholesky(system)  5.05 us
    another operation x2, other arithmetic, body(): lax.linalg.triangular_solve(cholesky_factor, middle, left_side=True, lowe...  4.32 us
  transfers between devices with their start and end apart: 2, of which 0 were waited for; matrix products, arithmetic and copies ran while one was open for 13% of the time, Pallas kernels for 0%

profile of v1, /device:TPU:0, one launch (start us, length us, event | category | flops | bytes accessed | tf_op | source)
XLA Modules:
  0.0 188.1 jit_solution(14125661927677147584)
XLA Ops:
  6.5 2.3 %stack.2 = bf16[16,48,1024]{2,1,0:T(8,128)(2,1)} broadcast(bf16[48,1024]{1,0:T(8,128)(2,1)} %param.10), dimensions={1,2} | broadcast | bytes 1671168 | tf_op jit(solution)/shard_map/stack | solution.py:21
  8.8 8.0 %all-to-all-start = ((bf16[16,48,1024]{2,1,0:T(8,128)(2,1)}), bf16[16,48,1024]{2,1,0:T(8,128)(2,1)S(1)}, u32[]{:S(2)}, u32[]{:S(2)}) async-start(bf16[16,48,1024]{2,1,0:T(8,128)(2,1)} %stack.2), calls=%async_computation | async-start | bytes 3145728 | tf_op jit(solution)/shard_map/all_to_all | solution.py:21
  16.8 0.0 reduce-scatter.2.cloned.1.call-start
  16.9 0.7 compare_select_fusion
  17.5 0.7 compare_select_fusion.1
  18.2 14.1 %all_gather.3 = bf16[48,8192]{1,0:T(8,128)(2,1)S(1)} all-gather(bf16[48,1024]{1,0:T(8,128)(2,1)} %param.11), channel_id=1, replica_groups=mesh['row'=8,'col'=16] {'row'}, dimensions={1}, use_global_device_ids=true | all-gather | bytes 884736 | tf_op jit(solution)/shard_map/all_gather | solution.py:23
  32.3 0.1 copy_bitcast_fusion.1
  32.4 0.6 gather_fusion
  33.0 0.7 broadcast_subtract_fusion
  33.7 12.1 %fusion.6 = f32[4,48,128,128]{3,1,2,0:T(8,128)} fusion(bf16[4,128,128,128]{3,2,1,0:T(8,128)(2,1)} %param.6, bf16[4,48,128]{2,1,0:T(8,128)(2,1)S(1)} %gather_fusion), kind=kOutput, calls=%fused_computation.10 | convolution fusion | flops 805306368 | bytes 29409280 | tf_op jit(solution)/shard_map/trc,tabc->trab/dot_general | solution.py:30
  45.8 0.0 all-to-all-done
  45.8 0.9 copy.15
  46.6 0.7 reshape_reshape.3
  47.4 1.0 copy.16
  48.4 0.6 gather_fusion.1
  49.0 0.0 copy-start
  49.0 0.0 copy-start.1
  49.0 16.7 %fusion = f32[4,48,1,128]{3,2,1,0:T(1,128)S(1)} fusion(f32[4,48,128,128]{3,1,2,0:T(8,128)} %fusion.6, bf16[4,48,128,1]{2,1,0,3:T(8,128)(2,1)S(1)} %bitcast.44), kind=kOutput, calls=%fused_computation.2 | convolution fusion | flops 37748736 | bytes 12730368 | tf_op jit(solution)/shard_map/trab,trb->tra/dot_general | solution.py:33
  65.7 1.5 fusion.2
  67.2 3.5 %copy.33 = f32[6,8,128,128]{3,1,2,0:T(8,128)} copy(f32[6,8,128,128]{3,2,1,0:T(8,128)S(1)} %bitcast.42) | data formatting | bytes 6291456
  70.7 0.0 reduce-scatter.2.cloned.1.call-update
  70.7 0.1 fusion.17
  70.9 74.9 %psum.14 = f32[48,48]{1,0:T(8,128)S(1)} all-reduce(f32[48,48]{1,0:T(8,128)S(1)} %fusion.17), channel_id=1, replica_groups=mesh['row'=8,'col'=16] {'col'}, use_global_device_ids=true, to_apply=%region_0.0 | all-reduce | flops 2304 | bytes 18432 | tf_op jit(solution)/shard_map/psum | solution.py:13
  145.7 0.1 fusion.18
  145.9 23.6 %psum.15 = f32[48,48]{1,0:T(8,128)S(1)} all-reduce(f32[48,48]{1,0:T(8,128)S(1)} %fusion.18), channel_id=1, replica_groups=mesh['row'=8,'col'=16] {'row'}, use_global_device_ids=true, to_apply=%region_1.0 | all-reduce | flops 2304 | bytes 18432 | tf_op jit(solution)/shard_map/psum | solution.py:16
  169.5 0.1 copy.13
  169.6 4.4 %cholesky.16 = f32[48,48]{1,0:T(8,128)S(1)} custom-call(f32[48,48]{1,0:T(8,128)S(1)} %fusion.13), custom_call_target="Cholesky" | custom-call | tf_op jit(solution)/shard_map/jit(cholesky)/cholesky | solution.py:45
  174.0 0.6 compare_reduce_fusion
  174.6 0.7 fusion.8
  175.3 3.7 %custom-call.8 = f32[1,48,48]{1,2,0:T(8,128)S(1)} custom-call(f32[1,48,48]{2,1,0:T(8,128)S(1)} %fusion.8), custom_call_target="InvertDiagBlocksLowerTriangular" | custom-call | tf_op jit(solution)/shard_map/triangular_solve | solution.py:47
  179.0 1.3 fusion.11
  180.3 1.0 fusion.9
  (8 shorter events, 0.1 us)
Async XLA Ops:
  8.8 36.9 %all-to-all-start = ((bf16[16,48,1024]{2,1,0:T(8,128)(2,1)}), bf16[16,48,1024]{2,1,0:T(8,128)(2,1)S(1)}, u32[]{:S(2)}, u32[]{:S(2)}) async-start(bf16[16,48,1024]{2,1,0:T(8,128)(2,1)} %stack.2), calls=%async_computation | async-start | bytes 3145728 | tf_op jit(solution)/shard_map/all_to_all | solution.py:21
  16.8 162.2 %reduce-scatter.2.cloned.1.call-start = ((), (), s32[]{:S(2)}) async-start(), calls=%async_computation.2 | async-start | bytes 3342336 | tf_op jit(solution)/shard_map/reduce_scatter | solution.py:44
  49.0 21.7 %copy-start = (bf16[48,1024]{1,0:T(8,128)(2,1)S(1)}, bf16[48,1024]{1,0:T(8,128)(2,1)}, u32[]{:S(2)}) copy-start(bf16[48,1024]{1,0:T(8,128)(2,1)} %param.10) | copy-start | bytes 294916
  49.0 96.7 %copy-start.1 = (bf16[48,1024]{1,0:T(8,128)(2,1)S(1)}, bf16[48,1024]{1,0:T(8,128)(2,1)}, u32[]{:S(2)}) copy-start(bf16[48,1024]{1,0:T(8,128)(2,1)} %param.11) | copy-start | bytes 294916
Sparse Core Ops, SparseCore 0:
  70.8 77.7 reduce-scatter.1

commit v2 on v0

--- a/solution.py
+++ b/solution.py
@@ -13,8 +13,11 @@
     gram_two = lax.psum(
         jnp.dot(factor_mode2, factor_mode2.T, preferred_element_type=jnp.float32), "col"
     )
-    gram_three = lax.psum(
-        jnp.dot(factor_mode3, factor_mode3.T, preferred_element_type=jnp.float32), "row"
+    gram_three = jnp.sum(
+        lax.all_gather(
+            jnp.dot(factor_mode3, factor_mode3.T, preferred_element_type=jnp.float32), "row"
+        ),
+        axis=0,
     )
     system = gram_two * gram_three + ridge_term * jnp.eye(rank_count, dtype=jnp.float32)
     full_two = lax.all_gather(factor_mode2, "col", axis=1, tiled=True)

time: 195 us -> 184 us (0.944)
  blocking collectives: 110 us -> 99.5 us
    psum x1 -> x0, blocking collectives: 23.6 us -> none  [body(): lax.psum(jnp.dot(factor_mode3, factor_mode3.T, preferred_element_type=jnp...]
    all_gather x0 -> x1, blocking collectives: none -> 13.1 us  [body(): lax.all_gather(jnp.dot(factor_mode3, factor_mode3.T, preferred_element_ty...]
where the time goes in v2:
time: 184 us
  blocking collectives  99.5 us (54%)
  matrix products  32.8 us (18%)
  waiting for transfers between devices  20.3 us (11%)
  between operations  13.5 us (7%)
  other arithmetic  11.4 us (6%)
  local copies, waits for them, and re-layouts  6.48 us (4%)
    psum x1, blocking collectives, body(): lax.psum(jnp.dot(factor_mode2, factor_mode2.T, preferred_element_type=jnp...  72.2 us
    all_gather x1, waiting for transfers between devices, body(): full_two = lax.all_gather(factor_mode2, 'col', axis=1, tiled=True)  19.6 us
    dot_general x1, matrix products, body(): jnp.einsum('trab,trb->tra', contracted, mode2_rows.astype(jnp.float32), p...  16.7 us
    all_gather x1, blocking collectives, body(): full_three = lax.all_gather(factor_mode3, 'row', axis=1, tiled=True)  14.2 us
    all_gather x1, blocking collectives, body(): lax.all_gather(jnp.dot(factor_mode3, factor_mode3.T, preferred_element_ty...  13.1 us
    dot_general x1, matrix products, body(): jnp.einsum('trc,tabc->trab', mode3_rows, tensor_tiles, preferred_element_...  12.1 us
    another operation x3, other arithmetic, body(): cholesky_factor = jnp.linalg.cholesky(system)  5.05 us
    another operation x2, other arithmetic, body(): lax.linalg.triangular_solve(cholesky_factor, middle, left_side=True, lowe...  4.32 us
  transfers between devices with their start and end apart: 2, of which 1 were waited for; matrix products, arithmetic and copies ran while one was open for 13% of the time, Pallas kernels for 0%

profile of v2, /device:TPU:0, one launch (start us, length us, event | category | flops | bytes accessed | tf_op | source)
XLA Modules:
  0.0 184.1 jit_solution(9080652229406300847)
XLA Ops:
  6.5 0.0 all-gather.3.cloned.1.call-start
  6.5 0.7 all-gather.3.cloned.1.call-update
  7.3 0.0 reduce-scatter.2.cloned.1.call-start
  7.3 0.7 compare_select_fusion.1
  8.0 14.2 %all_gather.14 = bf16[48,8192]{1,0:T(8,128)(2,1)S(1)} all-gather(bf16[48,1024]{1,0:T(8,128)(2,1)} %param.11), channel_id=1, replica_groups=mesh['row'=8,'col'=16] {'row'}, dimensions={1}, use_global_device_ids=true | all-gather | bytes 884736 | tf_op jit(solution)/shard_map/all_gather | solution.py:24
  22.2 0.1 copy_bitcast_fusion.2
  22.3 0.6 gather_fusion
  22.9 0.7 compare_select_fusion
  23.6 0.7 broadcast_subtract_fusion
  24.2 12.1 %fusion.6 = f32[4,48,128,128]{3,1,2,0:T(8,128)} fusion(bf16[4,128,128,128]{3,2,1,0:T(8,128)(2,1)} %param.6, bf16[4,48,128]{2,1,0:T(8,128)(2,1)S(1)} %gather_fusion), kind=kOutput, calls=%fused_computation.11 | convolution fusion | flops 805306368 | bytes 29409280 | tf_op jit(solution)/shard_map/trc,tabc->trab/dot_general | solution.py:31
  36.3 19.6 %all-gather.3.cloned.1.call-done = bf16[48,16384]{1,0:T(8,128)(2,1)} async-done(((bf16[48,1024]{1,0:T(8,128)(2,1)}), bf16[48,16384]{1,0:T(8,128)(2,1)}) %all-gather.3.cloned.1.call-update) | async-done | bytes 1572880 | tf_op jit(solution)/shard_map/all_gather | solution.py:23
  55.9 1.7 copy_bitcast_fusion.1
  57.6 0.6 gather_fusion.1
  58.1 0.0 copy-start
  58.1 0.0 copy-start.1
  58.2 16.7 %fusion = f32[4,48,1,128]{3,2,1,0:T(1,128)S(1)} fusion(f32[4,48,128,128]{3,1,2,0:T(8,128)} %fusion.6, bf16[4,48,128,1]{2,1,0,3:T(8,128)(2,1)S(1)} %bitcast.49), kind=kOutput, calls=%fused_computation.2 | convolution fusion | flops 37748736 | bytes 12730368 | tf_op jit(solution)/shard_map/trab,trb->tra/dot_general | solution.py:34
  74.9 1.5 fusion.2
  76.4 3.5 %copy.30 = f32[6,8,128,128]{3,1,2,0:T(8,128)} copy(f32[6,8,128,128]{3,2,1,0:T(8,128)S(1)} %bitcast.47) | data formatting | bytes 6291456
  79.8 0.0 reduce-scatter.2.cloned.1.call-update
  79.9 0.0 copy-done
  79.9 0.1 fusion.18
  80.0 13.1 %all-gather = f32[384,48]{1,0:T(8,128)S(1)} all-gather(f32[48,48]{1,0:T(8,128)S(1)} %fusion.18), channel_id=2, replica_groups=mesh['row'=8,'col'=16] {'row'}, dimensions={0}, use_global_device_ids=true | all-gather | bytes 82944 | tf_op jit(solution)/shard_map/all_gather | solution.py:17
  93.2 0.0 copy-done.1
  93.2 0.1 fusion.17
  93.3 72.2 %psum.7 = f32[48,48]{1,0:T(8,128)S(1)} all-reduce(f32[48,48]{1,0:T(8,128)S(1)} %fusion.17), channel_id=1, replica_groups=mesh['row'=8,'col'=16] {'col'}, use_global_device_ids=true, to_apply=%region_0.0 | all-reduce | flops 2304 | bytes 18432 | tf_op jit(solution)/shard_map/psum | solution.py:13
  165.5 0.1 copy.9
  165.6 4.4 %cholesky.16 = f32[48,48]{1,0:T(8,128)S(1)} custom-call(f32[48,48]{1,0:T(8,128)S(1)} %fusion.13), custom_call_target="Cholesky" | custom-call | tf_op jit(solution)/shard_map/jit(cholesky)/cholesky | solution.py:46
  170.0 0.6 compare_reduce_fusion
  170.7 0.7 fusion.8
  171.3 3.7 %custom-call.8 = f32[1,48,48]{1,2,0:T(8,128)S(1)} custom-call(f32[1,48,48]{2,1,0:T(8,128)S(1)} %fusion.8), custom_call_target="InvertDiagBlocksLowerTriangular" | custom-call | tf_op jit(solution)/shard_map/triangular_solve | solution.py:48
  175.0 1.3 fusion.11
  176.3 1.0 fusion.9
  (7 shorter events, 0.1 us)
Async XLA Ops:
  6.5 49.4 %all-gather.3.cloned.1.call-start = ((), (), s32[]{:S(2)}) async-start(), calls=%async_computation.1 | async-start | bytes 1671168 | tf_op jit(solution)/shard_map/all_gather | solution.py:23
  7.3 167.8 %reduce-scatter.2.cloned.1.call-start = ((), (), s32[]{:S(2)}) async-start(), calls=%async_computation.2 | async-start | bytes 3342336 | tf_op jit(solution)/shard_map/reduce_scatter | solution.py:45
  58.1 21.7 %copy-start = (bf16[48,1024]{1,0:T(8,128)(2,1)S(1)}, bf16[48,1024]{1,0:T(8,128)(2,1)}, u32[]{:S(2)}) copy-start(bf16[48,1024]{1,0:T(8,128)(2,1)} %param.11) | copy-start | bytes 294916
  58.1 35.0 %copy-start.1 = (bf16[48,1024]{1,0:T(8,128)(2,1)S(1)}, bf16[48,1024]{1,0:T(8,128)(2,1)}, u32[]{:S(2)}) copy-start(bf16[48,1024]{1,0:T(8,128)(2,1)} %param.10) | copy-start | bytes 294916
Sparse Core Ops, SparseCore 0:
  9.5 46.3 all-gather.2
  80.0 75.9 reduce-scatter.1
